TPU v7x, 128 devices: a whole 4x4x4 slice. The times are simulated.
128 devices in a mesh: view: 4 (over y), tile: 32 (over z, x, core).
Axes of the slice: x: 4, y: 4, z: 4, core: 2. Of those that a mesh axis runs over, the one named last changes fastest.
Arguments:
- estimate: float32 [128, 768, 512], P(None, 'tile'), may hold values from 0.5 to 2
- view_stacks: float32 [4, 128, 768, 512], P('view', 'tile'), may hold values from 0 to 4
- profile_z: float32 [4, 31], P('view'), may hold values from 0.2 to 1
- profile_y: float32 [4, 15], P('view'), may hold values from 0.2 to 1
- profile_x: float32 [4, 15], P('view'), may hold values from 0.2 to 1
- offsets: int32 [4], P('view'), may hold values from -16 to 16, as said below
- coverage: int32 [32, 4], P('tile'), may hold values from 0 to 1, as said below
Outputs:
- new_estimate: float32 [128, 768, 512], P(None, 'tile')
Inputs may be any that keep to these rules, and one draw needn't show every extreme that they name: `offsets`: some view has offset 16 and some view has offset -16. `coverage`: every tile is intersected by at least one view.
All inputs are finite; a program needn't handle non-finite values.
Results may differ from a plain program's by a relative error of at most 0.0001.
Values sent between devices are 32-bit elements; how exact they have to be, the bound alone decides.
A program may use at most 192 MiB of HBM per device.

v0:
```python
import jax
import jax.numpy as jnp
from jax import lax
from jax.sharding import PartitionSpec as P

MAXOFF = 16


def with_halo(cells, sides, width):
    for axis, dim in sides:
        count = lax.axis_size(axis)
        ends = count - 1
        head = lax.slice_in_dim(cells, 0, width, axis=dim)
        tail = lax.slice_in_dim(cells, cells.shape[dim] - width, cells.shape[dim], axis=dim)
        cells = jnp.concatenate(
            [
                lax.ppermute(tail, axis, [(i, (i + 1) % count) for i in range(ends)]),
                cells,
                lax.ppermute(head, axis, [((i + 1) % count, i) for i in range(ends)]),
            ],
            axis=dim,
        )
    return cells


def band_matrix(kernel, rows_out):
    taps_count = kernel.shape[0]
    rows_in = rows_out + taps_count - 1
    out_index = jnp.arange(rows_out, dtype=jnp.int32)
    in_index = jnp.arange(rows_in, dtype=jnp.int32)
    distance = in_index[None, :] - out_index[:, None]
    tap_index = jnp.arange(taps_count, dtype=jnp.int32)
    hits = (distance[None, :, :] == tap_index[:, None, None]).astype(jnp.float32)
    return jnp.sum(hits * kernel[:, None, None], axis=0)


def band_blur(field, kernel, along):
    highest = lax.Precision.HIGHEST
    taps_count = kernel.shape[0]
    half = (taps_count - 1) // 2
    extent = field.shape[along]
    block = min(128, extent)
    count = extent // block
    widths = [(0, 0), (0, 0), (0, 0)]
    widths[along] = (half, block - half)
    padded = jnp.pad(field, widths)
    band = band_matrix(kernel, block)
    head_band = band[:, :block]
    tail_band = band[:, block:]
    head = lax.slice_in_dim(padded, 0, count * block, axis=along)
    tail = lax.slice_in_dim(padded, block, (count + 1) * block, axis=along)
    if along == 0:
        head = head.reshape((count, block) + field.shape[1:])
        tail = tail.reshape((count, block) + field.shape[1:])[:, : taps_count - 1]
        result = jnp.einsum(
            "jbyx,ob->joyx", head, head_band, precision=highest, preferred_element_type=jnp.float32
        )
        result = result + jnp.einsum(
            "jbyx,ob->joyx", tail, tail_band, precision=highest, preferred_element_type=jnp.float32
        )
        return result.reshape(field.shape)
    head = head.reshape(field.shape[:2] + (count, block))
    tail = tail.reshape(field.shape[:2] + (count, block))[..., : taps_count - 1]
    result = jnp.einsum(
        "zyjb,ob->zyjo", head, head_band, precision=highest, preferred_element_type=jnp.float32
    )
    result = result + jnp.einsum(
        "zyjb,ob->zyjo", tail, tail_band, precision=highest, preferred_element_type=jnp.float32
    )
    return result.reshape(field.shape)


def blur_rows(field, matrix_y, weights_z, weights_x):
    highest = lax.Precision.HIGHEST
    result = band_blur(field, weights_z, 0)
    result = jnp.einsum(
        "ya,zax->zyx", matrix_y, result, precision=highest, preferred_element_type=jnp.float32
    )
    return band_blur(result, weights_x, 2)


def on_device(estimate, view_stacks, profile_z, profile_y, profile_x, offsets, coverage):
    weights_z = profile_z[0] / jnp.sum(profile_z[0])
    weights_y = profile_y[0] / jnp.sum(profile_y[0])
    weights_x = profile_x[0] / jnp.sum(profile_x[0])
    row_count = estimate.shape[1]
    x_cells = estimate.shape[2]
    half_y = (weights_y.shape[0] - 1) // 2
    padded = jnp.pad(view_stacks[0], ((0, 0), (0, 0), (MAXOFF, MAXOFF)))
    shifted = lax.dynamic_slice_in_dim(padded, MAXOFF + offsets[0], x_cells, 2)
    stacked = lax.all_to_all(shifted, "tile", split_axis=1, concat_axis=0, tiled=True)
    flipped = weights_y[::-1]
    back_z = weights_z[::-1]
    back_x = weights_x[::-1]
    estimate_ext = with_halo(estimate, (("tile", 1),), half_y)
    blurred = blur_rows(estimate_ext, band_matrix(weights_y, row_count), weights_z, weights_x)
    quotient = stacked / blurred
    quotient_ext = with_halo(quotient, (("tile", 1),), half_y)
    back_blur = blur_rows(quotient_ext, band_matrix(flipped, row_count), back_z, back_x)
    view_index = lax.axis_index("view")
    covered = lax.dynamic_index_in_dim(coverage[0], view_index, 0, keepdims=False).astype(
        jnp.float32
    )
    view_count = jnp.sum(coverage[0]).astype(jnp.float32)
    weighted = covered * back_blur
    summed = lax.psum(weighted, "view")
    return estimate * summed / view_count


def solution(mesh):
    return jax.shard_map(
        on_device,
        mesh=mesh,
        in_specs=(
            P(None, "tile", None),
            P("view", "tile", None, None),
            P("view", None),
            P("view", None),
            P("view", None),
            P("view"),
            P("tile", None),
        ),
        out_specs=P(None, "tile", None),
        check_vma=False,
    )
```

profile of v0, /device:TPU:1, one launch (start us, length us, event | category | flops | bytes accessed | tf_op | source)
XLA Modules:
  0.0 461.1 jit_solution(2243969198912554570)
XLA Ops:
  6.5 6.4 %copy.65 = f32[128,24,512]{2,0,1:T(8,128)S(1)} copy(f32[128,24,512]{2,1,0:T(8,128)} %param.7) | data formatting | bytes 12582912 | tf_op args[0]
  13.0 2.7 copy-done
  15.7 2.2 fusion.39
  17.9 4.7 %collective-permute-start = (f32[128,7,512]{2,0,1:T(8,128)}, f32[128,7,512]{2,0,1:T(8,128)S(1)}, u32[]{:S(2)}, u32[]{:S(2)}) collective-permute-start(f32[128,7,512]{2,0,1:T(8,128)} %get-tuple-element.17), channel_id=1, source_target_pairs={{0,1},{1,2},{2,3},{3,4},{4,5},{5,6},{6,7},{7,8},{8,9},{9,10},{10,1... | collective-permute-start | bytes 5505032 | tf_op jit(solution)/shard_map/ppermute | solution.py:17
  22.7 2.1 collective-permute-start.1
  25.4 6.7 %copy.107 = f32[1,4,768,512]{3,1,2,0:T(4,128)} copy(f32[1,4,768,512]{3,2,1,0:T(8,128)S(1)} %copy-done.4) | data formatting | bytes 12582912 | tf_op args[1]
  32.1 8.7 %pad_dynamic-slice_fusion = f32[4,768,512]{2,0,1:T(4,128)} fusion(s32[]{:T(128)S(6)} %select_n.8, f32[4,768,512]{2,0,1:T(4,128)} %bitcast.76), kind=kLoop, calls=%fused_computation.21 | loop fusion | bytes 12582916 | tf_op jit(solution)/shard_map/dynamic_slice | solution.py:90
  40.9 8.7 %all-to-all-start = ((f32[4,768,512]{2,0,1:T(4,128)}), f32[4,768,512]{2,0,1:T(4,128)}, u32[]{:S(2)}, u32[]{:S(2)}) async-start(f32[4,768,512]{2,0,1:T(4,128)} %pad_dynamic-slice_fusion), calls=%async_computation | async-start | bytes 12582912 | tf_op jit(solution)/shard_map/all_to_all | solution.py:91
  50.1 0.6 reduce_sum.90
  50.8 0.6 reduce_sum.93
  51.5 0.6 reduce_sum.95
  52.2 0.6 broadcast_divide_fusion.2
  53.8 0.6 broadcast_divide_fusion.4
  55.0 11.0 %select_maximum_fusion.2 = f32[256,38,512]{2,0,1:T(8,128)} fusion(f32[128,7,512]{2,0,1:T(8,128)} %collective-permute-done.1, f32[128,24,512]{2,0,1:T(8,128)} %copy-done, f32[128,7,512]{2,0,1:T(8,128)S(1)} %collective-permute-done), kind=kLoop, calls=%fused_computation.4 | loop fusion | flops 39845888 | bytes 29884416 | tf_op jit(solution)/shard_map/concatenate | solution.py:15
  66.0 9.5 %slice_bitcast_fusion.1 = f32[1,128,38,512]{3,1,2,0:T(8,128)} fusion(f32[256,38,512]{2,0,1:T(8,128)} %select_maximum_fusion.2), kind=kLoop, calls=%fused_computation.14 | loop fusion | bytes 19922944 | tf_op jit(solution)/shard_map/reshape | solution.py:54
  75.5 9.8 %fusion.31 = f32[128,38,512]{2,0,1:T(8,128)S(1)} fusion(f32[1,128,38,512]{3,1,2,0:T(8,128)} %slice_bitcast_fusion.1, f32[128,158]{0,1:T(8,128)S(1)} %get-tuple-element.6), kind=kOutput, calls=%fused_computation.41 | convolution fusion | flops 896532480 | bytes 12468224 | tf_op jit(solution)/shard_map/jbyx,ob->joyx/dot_general | solution.py:58
  85.3 15.1 %fusion.13 = f32[128,38,512]{2,0,1:T(8,128)S(1)} fusion(f32[128,38,512]{2,0,1:T(8,128)S(1)} %fusion.31, f32[256,38,512]{2,0,1:T(8,128)} %select_maximum_fusion.2, f32[128,158]{0,1:T(8,128)S(1)} %get-tuple-element.6), kind=kOutput, calls=%fused_computation.30 | convolution fusion | flops 3827695616 | bytes 29949952 | tf_op jit(solution)/shard_map/jbyx,ob->joyx/dot_general | solution.py:55
  100.4 18.2 %fusion.24 = f32[128,24,512]{2,1,0:T(8,128)S(1)} fusion(f32[128,38,512]{2,0,1:T(8,128)S(1)} %fusion.13, f32[24,38]{1,0:T(8,128)S(1)} %get-tuple-element.10), kind=kOutput, calls=%fused_computation.33 | convolution fusion | flops 717225984 | bytes 16256576 | tf_op jit(solution)/shard_map/ya,zax->zyx/dot_general | solution.py:76
  118.6 6.4 %pad_slice_fusion.3 = (f32[128,24,512]{2,1,0:T(8,128)}, f32[128,24,512]{2,1,0:T(8,128)}) fusion(f32[128,24,512]{2,1,0:T(8,128)S(1)} %fusion.24), kind=kLoop, calls=%fused_computation.20 | loop fusion | bytes 18874368 | tf_op jit(solution)/shard_map/slice | solution.py:50
  125.0 6.6 %copy.83 = f32[128,24,512]{0,2,1:T(8,128)} copy(f32[128,24,512]{2,1,0:T(8,128)} %get-tuple-element.16) | data formatting | bytes 12582912 | tf_op jit(solution)/shard_map/reshape | solution.py:63
  131.6 7.6 %reshape.113 = f32[128,24,4,128]{3,2,1,0:T(4,128)} reshape(f32[128,24,512]{2,1,0:T(8,128)} %get-tuple-element.15) | data formatting | bytes 12582912 | tf_op jit(solution)/shard_map/reshape | solution.py:62
  139.1 6.5 %fusion.34 = f32[128,24,4,128]{0,3,2,1:T(8,128)S(1)} fusion(f32[128,24,4,128]{0,3,2,1:T(8,128)} %bitcast.84, f32[128,142]{0,1:T(8,128)S(1)} %get-tuple-element.8), kind=kOutput, calls=%fused_computation.47 | convolution fusion | flops 264241152 | bytes 7086080 | tf_op jit(solution)/shard_map/zyjb,ob->zyjo/dot_general | solution.py:67
  145.6 10.5 %fusion.19 = f32[128,24,4,128]{0,3,2,1:T(8,128)} fusion(f32[128,24,4,128]{0,3,2,1:T(8,128)S(1)} %fusion.34, f32[128,24,4,128]{3,2,1,0:T(4,128)S(1)} %copy-done.3, f32[128,142]{0,1:T(8,128)S(1)} %get-tuple-element.8), kind=kOutput, calls=%fused_computation.32 | convolution fusion | flops 2417491968 | bytes 18939904 | tf_op jit(solution)/shard_map/zyjb,ob->zyjo/dot_general | solution.py:64
  156.1 6.6 %copy.73 = f32[128,24,512]{2,0,1:T(8,128)} copy(f32[128,24,512]{0,2,1:T(8,128)} %bitcast.81) | data formatting | bytes 12582912 | tf_op jit(solution)/shard_map/reshape | solution.py:70
  162.7 5.0 %copy.62 = f32[4,768,512]{2,1,0:T(8,128)S(1)} copy(f32[4,768,512]{2,0,1:T(4,128)} %all-to-all-done) | data formatting | bytes 12582912 | tf_op jit(solution)/shard_map/all_to_all | solution.py:91
  167.6 1.0 copy.63
  169.2 4.2 copy_divide_fusion
  173.5 2.7 copy-done.1
  176.2 2.2 fusion.38
  178.3 3.5 collective-permute-start.2
  181.9 1.9 collective-permute-start.3
  183.8 0.6 fusion.40
  184.4 17.9 %collective-permute-done.2 = f32[128,7,512]{2,0,1:T(8,128)S(1)} collective-permute-done((f32[128,7,512]{2,0,1:T(8,128)}, f32[128,7,512]{2,0,1:T(8,128)S(1)}, u32[]{:S(2)}, u32[]{:S(2)}) %collective-permute-start.2) | collective-permute-done | bytes 1835040 | tf_op jit(solution)/shard_map/ppermute | solution.py:17
  202.3 4.4 collective-permute-done.3
  206.7 11.2 %select_maximum_fusion = f32[256,38,512]{2,0,1:T(8,128)} fusion(f32[128,7,512]{2,0,1:T(8,128)} %collective-permute-done.3, f32[128,24,512]{2,0,1:T(8,128)} %copy-done.1, f32[128,7,512]{2,0,1:T(8,128)S(1)} %collective-permute-done.2), kind=kLoop, calls=%fused_computation.2 | loop fusion | flops 39845888 | bytes 29884416 | tf_op jit(solution)/shard_map/concatenate | solution.py:15
  217.9 9.5 %slice_bitcast_fusion = f32[1,128,38,512]{3,1,2,0:T(8,128)} fusion(f32[256,38,512]{2,0,1:T(8,128)} %select_maximum_fusion), kind=kLoop, calls=%fused_computation.11 | loop fusion | bytes 19922944 | tf_op jit(solution)/shard_map/reshape | solution.py:54
  227.5 9.8 %fusion.30 = f32[128,38,512]{2,0,1:T(8,128)S(1)} fusion(f32[1,128,38,512]{3,1,2,0:T(8,128)} %slice_bitcast_fusion, f32[128,158]{0,1:T(8,128)S(1)} %get-tuple-element.5), kind=kOutput, calls=%fused_computation.39 | convolution fusion | flops 896532480 | bytes 12468224 | tf_op jit(solution)/shard_map/jbyx,ob->joyx/dot_general | solution.py:58
  237.2 15.5 %fusion.16 = f32[128,38,512]{2,0,1:T(8,128)S(1)} fusion(f32[128,38,512]{2,0,1:T(8,128)S(1)} %fusion.30, f32[256,38,512]{2,0,1:T(8,128)} %select_maximum_fusion, f32[128,158]{0,1:T(8,128)S(1)} %get-tuple-element.5), kind=kOutput, calls=%fused_computation.31 | convolution fusion | flops 3827695616 | bytes 29949952 | tf_op jit(solution)/shard_map/jbyx,ob->joyx/dot_general | solution.py:55
  252.7 18.0 %fusion.27 = f32[128,24,512]{2,1,0:T(8,128)S(1)} fusion(f32[128,38,512]{2,0,1:T(8,128)S(1)} %fusion.16, f32[24,38]{1,0:T(8,128)S(1)} %get-tuple-element.9), kind=kOutput, calls=%fused_computation.34 | convolution fusion | flops 717225984 | bytes 16256576 | tf_op jit(solution)/shard_map/ya,zax->zyx/dot_general | solution.py:76
  270.8 6.4 %pad_slice_fusion.1 = (f32[128,24,512]{2,1,0:T(8,128)}, f32[128,24,512]{2,1,0:T(8,128)}) fusion(f32[128,24,512]{2,1,0:T(8,128)S(1)} %fusion.27), kind=kLoop, calls=%fused_computation.18 | loop fusion | bytes 18874368 | tf_op jit(solution)/shard_map/slice | solution.py:50
  277.2 6.6 %copy.84 = f32[128,24,512]{0,2,1:T(8,128)} copy(f32[128,24,512]{2,1,0:T(8,128)} %get-tuple-element.12) | data formatting | bytes 12582912 | tf_op jit(solution)/shard_map/reshape | solution.py:63
  283.7 7.6 %reshape.118 = f32[128,24,4,128]{3,2,1,0:T(4,128)} reshape(f32[128,24,512]{2,1,0:T(8,128)} %get-tuple-element.11) | data formatting | bytes 12582912 | tf_op jit(solution)/shard_map/reshape | solution.py:62
  291.3 6.5 %fusion.32 = f32[128,24,4,128]{0,3,2,1:T(8,128)S(1)} fusion(f32[128,24,4,128]{0,3,2,1:T(8,128)} %bitcast.83, f32[128,142]{0,1:T(8,128)S(1)} %get-tuple-element.7), kind=kOutput, calls=%fused_computation.45 | convolution fusion | flops 264241152 | bytes 7086080 | tf_op jit(solution)/shard_map/zyjb,ob->zyjo/dot_general | solution.py:67
  297.8 11.4 %add_multiply_fusion = f32[128,24,4,128]{0,3,2,1:T(8,128)} fusion(f32[128,24,4,128]{0,3,2,1:T(8,128)S(1)} %fusion.32, f32[]{:T(128)} %bitcast, f32[128,24,4,128]{3,2,1,0:T(4,128)S(1)} %copy-done.2, f32[128,142]{0,1:T(8,128)S(1)} %get-tuple-element.7), kind=kOutput, calls=%fused_computation.29 | convolution fusion | flops 2419064832 | bytes 18939908 | tf_op jit(solution)/shard_map/zyjb,ob->zyjo/dot_general | solution.py:64
  309.2 6.7 %copy.78 = f32[128,24,512]{2,1,0:T(8,128)} copy(f32[128,24,512]{0,2,1:T(8,128)} %bitcast.80) | data formatting | bytes 12582912 | tf_op jit(solution)/shard_map/mul | solution.py:105
  315.9 0.6 reduce_sum.99
  317.2 127.9 %all-reduce.7.cloned.1.call-done = f32[128,24,512]{2,1,0:T(8,128)} async-done(((f32[128,24,512]{2,1,0:T(8,128)}), f32[128,24,512]{2,1,0:T(8,128)}) %all-reduce.7.cloned.1.call-update) | async-done | bytes 6291472 | tf_op jit(solution)/shard_map/psum | solution.py:106
  445.1 8.9 %multiply_divide_fusion = f32[128,24,512]{2,1,0:T(8,128)} fusion(f32[128,24,512]{2,1,0:T(8,128)} %param.7, f32[128,24,512]{2,1,0:T(8,128)} %all-reduce.7.cloned.1.call-done, f32[]{:T(128)S(6)} %convert_element_type.25), kind=kLoop, calls=%fused_computation.28 | loop fusion | flops 3145728 | bytes 18874372 | tf_op jit(solution)/shard_map/div | solution.py:107
  (36 shorter events, 2.9 us)
Async XLA Ops:
  13.0 2.7 copy-start
  15.7 9.8 %copy-start.4 = (f32[1,4,768,512]{3,2,1,0:T(8,128)S(1)}, f32[1,4,768,512]{3,2,1,0:T(8,128)}, u32[]{:S(2)}) copy-start(f32[1,4,768,512]{3,2,1,0:T(8,128)} %param.8) | copy-start | bytes 18874372
  17.9 37.0 %collective-permute-start = (f32[128,7,512]{2,0,1:T(8,128)}, f32[128,7,512]{2,0,1:T(8,128)S(1)}, u32[]{:S(2)}, u32[]{:S(2)}) collective-permute-start(f32[128,7,512]{2,0,1:T(8,128)} %get-tuple-element.17), channel_id=1, source_target_pairs={{0,1},{1,2},{2,3},{3,4},{4,5},{5,6},{6,7},{7,8},{8,9},{9,10},{10,1... | collective-permute-start | bytes 5505032 | tf_op jit(solution)/shard_map/ppermute | solution.py:17
  22.7 32.3 %collective-permute-start.1 = (f32[128,7,512]{2,0,1:T(8,128)}, f32[128,7,512]{2,0,1:T(8,128)}, u32[]{:S(2)}, u32[]{:S(2)}) collective-permute-start(f32[128,7,512]{2,0,1:T(8,128)} %get-tuple-element.18), channel_id=1, source_target_pairs={{1,0},{2,1},{3,2},{4,3},{5,4},{6,5},{7,6},{8,7},{9,8},{10,9},{11,1... | collective-permute-start | bytes 5505032 | tf_op jit(solution)/shard_map/ppermute | solution.py:19
  40.9 9.2 %copy-start.7 = (f32[1,31]{1,0:T(1,128)S(1)}, f32[1,31]{1,0:T(1,128)}, u32[]{:S(2)}) copy-start(f32[1,31]{1,0:T(1,128)} %param.9) | copy-start | bytes 376
  40.9 9.9 %copy-start.5 = (f32[1,15]{1,0:T(1,128)S(1)}, f32[1,15]{1,0:T(1,128)}, u32[]{:S(2)}) copy-start(f32[1,15]{1,0:T(1,128)} %param.10) | copy-start | bytes 184
  40.9 10.6 %copy-start.6 = (f32[1,15]{1,0:T(1,128)S(1)}, f32[1,15]{1,0:T(1,128)}, u32[]{:S(2)}) copy-start(f32[1,15]{1,0:T(1,128)} %param.11) | copy-start | bytes 184
  40.9 121.8 %all-to-all-start = ((f32[4,768,512]{2,0,1:T(4,128)}), f32[4,768,512]{2,0,1:T(4,128)}, u32[]{:S(2)}, u32[]{:S(2)}) async-start(f32[4,768,512]{2,0,1:T(4,128)} %pad_dynamic-slice_fusion), calls=%async_computation | async-start | bytes 12582912 | tf_op jit(solution)/shard_map/all_to_all | solution.py:91
  49.6 395.5 %all-reduce.7.cloned.1.call-start = ((), (), s32[]{:S(2)}) async-start(), calls=%async_computation.1 | async-start | bytes 12582912 | tf_op jit(solution)/shard_map/psum | solution.py:106
  139.1 6.5 %copy-start.3 = (f32[128,24,4,128]{3,2,1,0:T(4,128)S(1)}, f32[128,24,4,128]{3,2,1,0:T(4,128)}, u32[]{:S(2)}) copy-start(f32[128,24,4,128]{3,2,1,0:T(4,128)} %reshape.113) | copy-start | bytes 18874372
  162.7 6.0 %slice-start = ((s8[6291456]{0:T(1024)(128)(4,1)}), s8[4194304]{0:T(1024)(128)(4,1)S(1)}, s32[]{:S(2)}) async-start(s8[6291456]{0:T(1024)(128)(4,1)} %bitcast.78), calls=%async_computation.2 | async-start | bytes 8388608
  167.6 1.6 slice-start.1
  173.5 2.7 copy-start.1
  176.2 7.6 %copy-start.8 = (s32[1,4]{1,0:T(1,128)S(1)}, s32[1,4]{1,0:T(1,128)}, u32[]{:S(2)}) copy-start(s32[1,4]{1,0:T(1,128)} %param.13) | copy-start | bytes 52
  178.3 24.0 %collective-permute-start.2 = (f32[128,7,512]{2,0,1:T(8,128)}, f32[128,7,512]{2,0,1:T(8,128)S(1)}, u32[]{:S(2)}, u32[]{:S(2)}) collective-permute-start(f32[128,7,512]{2,0,1:T(8,128)} %get-tuple-element.13), channel_id=1, source_target_pairs={{0,1},{1,2},{2,3},{3,4},{4,5},{5,6},{6,7},{7,8},{8,9},{9,10},{10,1... | collective-permute-start | bytes 5505032 | tf_op jit(solution)/shard_map/ppermute | solution.py:17
  181.9 24.9 %collective-permute-start.3 = (f32[128,7,512]{2,0,1:T(8,128)}, f32[128,7,512]{2,0,1:T(8,128)}, u32[]{:S(2)}, u32[]{:S(2)}) collective-permute-start(f32[128,7,512]{2,0,1:T(8,128)} %get-tuple-element.14), channel_id=1, source_target_pairs={{1,0},{2,1},{3,2},{4,3},{5,4},{6,5},{7,6},{8,7},{9,8},{10,9},{11,1... | collective-permute-start | bytes 5505032 | tf_op jit(solution)/shard_map/ppermute | solution.py:19
  291.3 6.5 %copy-start.2 = (f32[128,24,4,128]{3,2,1,0:T(4,128)S(1)}, f32[128,24,4,128]{3,2,1,0:T(4,128)}, u32[]{:S(2)}) copy-start(f32[128,24,4,128]{3,2,1,0:T(4,128)} %reshape.118) | copy-start | bytes 18874372
Sparse Core Ops, SparseCore 0:
  316.0 129.0 all-reduce.6
where the time goes:
time: 466 us; the launch traced here: 461 us
  waiting for transfers between devices  150 us (32%)
  matrix products  121 us (26%)
  local copies, waits for them, and re-layouts  112 us (24%)
  other arithmetic  41 us (9%)
  starting transfers between devices  21.5 us (5%)
  between operations  15.2 us (3%)
    psum x1, waiting for transfers between devices, on_device(): summed = lax.psum(weighted, 'view')  128 us
    dot_general x2, matrix products, blur_rows(): jnp.einsum('ya,zax->zyx', matrix_y, result, precision=highest, preferred_...  36.2 us
    dot_general x2, matrix products, band_blur(): jnp.einsum('jbyx,ob->joyx', head, head_band, precision=highest, preferred...  30.6 us
    concatenate x2, other arithmetic, with_halo(): jnp.concatenate([lax.ppermute(tail, axis, [(i, (i + 1) % count) for i in...  22.2 us
    dot_general x2, matrix products, band_blur(): jnp.einsum('zyjb,ob->zyjo', head, head_band, precision=highest, preferred...  21.9 us
    dot_general x2, matrix products, band_blur(): jnp.einsum('jbyx,ob->joyx', tail, tail_band, precision=highest, preferred...  19.5 us
    reshape x2, local copies, waits for them, and re-layouts, band_blur(): tail = tail.reshape((count, block) + field.shape[1:])[:, :taps_count - 1]  19.1 us
    unnamed x24, local copies, waits for them, and re-layouts  19.1 us
  transfers between devices with their start and end apart: 6, of which 3 were waited for; matrix products, arithmetic and copies ran while one was open for 28% of the time, Pallas kernels for 0%

commit v1 on v0

--- a/solution.py
+++ b/solution.py
@@ -103,7 +103,7 @@
     )
     view_count = jnp.sum(coverage[0]).astype(jnp.float32)
     weighted = covered * back_blur
-    summed = lax.psum(weighted, "view")
+    summed = jnp.sum(lax.all_gather(weighted, "view"), axis=0)
     return estimate * summed / view_count
 
 

time: 466 us -> 589 us (1.26)
  waiting for transfers between devices: 150 us -> 240 us
  local copies, waits for them, and re-layouts: 112 us -> 132 us
  other arithmetic: 41 us -> 53.6 us
    all_gather x0 -> x1, waiting for transfers between devices: none -> 218 us  [on_device(): summed = jnp.sum(lax.all_gather(weighted, 'view'), axis=0)]
    psum x1 -> x0, waiting for transfers between devices: 128 us -> none  [on_device(): summed = lax.psum(weighted, 'view')]
    reduce_sum x0 -> x1, other arithmetic: none -> 13.2 us  [on_device(): summed = jnp.sum(lax.all_gather(weighted, 'view'), axis=0)]
    unnamed x24 -> x26, local copies, waits for them, and re-layouts: 19.1 us -> 32.2 us
    div x0 -> x1, local copies, waits for them, and re-layouts: none -> 6.57 us  [on_device(): return estimate * summed / view_count]
  transfers between devices with their start and end apart: 6 -> 6, of which waited for: 3 -> 3; matrix products, arithmetic and copies ran while one was open for 28% -> 23% of each run, Pallas kernels for 0% -> 0%
where the time goes in v1:
time: 589 us; the launch traced here: 584 us
  waiting for transfers between devices  240 us (41%)
  local copies, waits for them, and re-layouts  132 us (22%)
  matrix products  121 us (21%)
  other arithmetic  53.6 us (9%)
  starting transfers between devices  21.6 us (4%)
  between operations  15.5 us (3%)
    all_gather x1, waiting for transfers between devices, on_device(): summed = jnp.sum(lax.all_gather(weighted, 'view'), axis=0)  218 us
    dot_general x2, matrix products, blur_rows(): jnp.einsum('ya,zax->zyx', matrix_y, result, precision=highest, preferred_...  36.2 us
    unnamed x26, local copies, waits for them, and re-layouts  32.2 us
    dot_general x2, matrix products, band_blur(): jnp.einsum('jbyx,ob->joyx', head, head_band, precision=highest, preferred...  30.6 us
    concatenate x2, other arithmetic, with_halo(): jnp.concatenate([lax.ppermute(tail, axis, [(i, (i + 1) % count) for i in...  22.2 us
    dot_general x2, matrix products, band_blur(): jnp.einsum('zyjb,ob->zyjo', head, head_band, precision=highest, preferred...  21.9 us
    dot_general x2, matrix products, band_blur(): jnp.einsum('jbyx,ob->joyx', tail, tail_band, precision=highest, preferred...  19.5 us
    reshape x2, local copies, waits for them, and re-layouts, band_blur(): tail = tail.reshape((count, block) + field.shape[1:])[:, :taps_count - 1]  19.1 us
  transfers between devices with their start and end apart: 6, of which 3 were waited for; matrix products, arithmetic and copies ran while one was open for 23% of the time, Pallas kernels for 0%

profile of v1, /device:TPU:1, one launch (start us, length us, event | category | flops | bytes accessed | tf_op | source)
XLA Modules:
  0.0 583.9 jit_solution(7412942745128743058)
XLA Ops:
  6.5 6.4 %copy.65 = f32[128,24,512]{2,0,1:T(8,128)S(1)} copy(f32[128,24,512]{2,1,0:T(8,128)} %param.7) | data formatting | bytes 12582912 | tf_op args[0]
  13.0 2.7 copy-done
  15.7 2.2 fusion.39
  17.9 4.7 collective-permute-start
  22.7 2.1 collective-permute-start.1
  25.5 6.7 %copy.111 = f32[1,4,768,512]{3,1,2,0:T(4,128)} copy(f32[1,4,768,512]{3,2,1,0:T(8,128)S(1)} %copy-done.4) | data formatting | bytes 12582912 | tf_op args[1]
  32.2 8.7 %pad_dynamic-slice_fusion = f32[4,768,512]{2,0,1:T(4,128)} fusion(s32[]{:T(128)S(6)} %select_n.8, f32[4,768,512]{2,0,1:T(4,128)} %bitcast.76), kind=kLoop, calls=%fused_computation.21 | loop fusion | bytes 12582916 | tf_op jit(solution)/shard_map/dynamic_slice | solution.py:90
  40.9 8.7 %all-to-all-start = ((f32[4,768,512]{2,0,1:T(4,128)}), f32[4,768,512]{2,0,1:T(4,128)}, u32[]{:S(2)}, u32[]{:S(2)}) async-start(f32[4,768,512]{2,0,1:T(4,128)} %pad_dynamic-slice_fusion), calls=%async_computation | async-start | bytes 12582912 | tf_op jit(solution)/shard_map/all_to_all | solution.py:91
  50.9 0.6 reduce_sum.102
  52.3 0.6 broadcast_divide_fusion.2
  55.1 11.0 %select_maximum_fusion.2 = f32[256,38,512]{2,0,1:T(8,128)} fusion(f32[128,7,512]{2,0,1:T(8,128)} %collective-permute-done.1, f32[128,24,512]{2,0,1:T(8,128)} %copy-done, f32[128,7,512]{2,0,1:T(8,128)S(1)} %collective-permute-done), kind=kLoop, calls=%fused_computation.4 | loop fusion | flops 39845888 | bytes 29884416 | tf_op jit(solution)/shard_map/concatenate | solution.py:15
  66.1 9.5 %slice_bitcast_fusion.1 = f32[1,128,38,512]{3,1,2,0:T(8,128)} fusion(f32[256,38,512]{2,0,1:T(8,128)} %select_maximum_fusion.2), kind=kLoop, calls=%fused_computation.14 | loop fusion | bytes 19922944 | tf_op jit(solution)/shard_map/reshape | solution.py:54
  75.6 9.8 %fusion.31 = f32[128,38,512]{2,0,1:T(8,128)S(1)} fusion(f32[1,128,38,512]{3,1,2,0:T(8,128)} %slice_bitcast_fusion.1, f32[128,158]{0,1:T(8,128)S(1)} %get-tuple-element.6), kind=kOutput, calls=%fused_computation.41 | convolution fusion | flops 896532480 | bytes 12468224 | tf_op jit(solution)/shard_map/jbyx,ob->joyx/dot_general | solution.py:58
  85.4 15.1 %fusion.13 = f32[128,38,512]{2,0,1:T(8,128)S(1)} fusion(f32[128,38,512]{2,0,1:T(8,128)S(1)} %fusion.31, f32[256,38,512]{2,0,1:T(8,128)} %select_maximum_fusion.2, f32[128,158]{0,1:T(8,128)S(1)} %get-tuple-element.6), kind=kOutput, calls=%fused_computation.30 | convolution fusion | flops 3827695616 | bytes 29949952 | tf_op jit(solution)/shard_map/jbyx,ob->joyx/dot_general | solution.py:55
  100.5 18.2 %fusion.24 = f32[128,24,512]{2,1,0:T(8,128)S(1)} fusion(f32[128,38,512]{2,0,1:T(8,128)S(1)} %fusion.13, f32[24,38]{1,0:T(8,128)S(1)} %get-tuple-element.10), kind=kOutput, calls=%fused_computation.33 | convolution fusion | flops 717225984 | bytes 16256576 | tf_op jit(solution)/shard_map/ya,zax->zyx/dot_general | solution.py:76
  118.7 6.4 %pad_slice_fusion.3 = (f32[128,24,512]{2,1,0:T(8,128)}, f32[128,24,512]{2,1,0:T(8,128)}) fusion(f32[128,24,512]{2,1,0:T(8,128)S(1)} %fusion.24), kind=kLoop, calls=%fused_computation.20 | loop fusion | bytes 18874368 | tf_op jit(solution)/shard_map/slice | solution.py:50
  125.1 6.6 %copy.86 = f32[128,24,512]{0,2,1:T(8,128)} copy(f32[128,24,512]{2,1,0:T(8,128)} %get-tuple-element.16) | data formatting | bytes 12582912 | tf_op jit(solution)/shard_map/reshape | solution.py:63
  131.7 7.6 %reshape.123 = f32[128,24,4,128]{3,2,1,0:T(4,128)} reshape(f32[128,24,512]{2,1,0:T(8,128)} %get-tuple-element.15) | data formatting | bytes 12582912 | tf_op jit(solution)/shard_map/reshape | solution.py:62
  139.2 6.5 %fusion.34 = f32[128,24,4,128]{0,3,2,1:T(8,128)S(1)} fusion(f32[128,24,4,128]{0,3,2,1:T(8,128)} %bitcast.84, f32[128,142]{0,1:T(8,128)S(1)} %get-tuple-element.8), kind=kOutput, calls=%fused_computation.47 | convolution fusion | flops 264241152 | bytes 7086080 | tf_op jit(solution)/shard_map/zyjb,ob->zyjo/dot_general | solution.py:67
  145.7 10.5 %fusion.19 = f32[128,24,4,128]{0,3,2,1:T(8,128)} fusion(f32[128,24,4,128]{0,3,2,1:T(8,128)S(1)} %fusion.34, f32[128,24,4,128]{3,2,1,0:T(4,128)S(1)} %copy-done.3, f32[128,142]{0,1:T(8,128)S(1)} %get-tuple-element.8), kind=kOutput, calls=%fused_computation.32 | convolution fusion | flops 2417491968 | bytes 18939904 | tf_op jit(solution)/shard_map/zyjb,ob->zyjo/dot_general | solution.py:64
  156.2 6.6 %copy.73 = f32[128,24,512]{2,0,1:T(8,128)} copy(f32[128,24,512]{0,2,1:T(8,128)} %bitcast.81) | data formatting | bytes 12582912 | tf_op jit(solution)/shard_map/reshape | solution.py:70
  162.8 5.0 copy.62
  167.7 1.0 copy.63
  169.3 4.2 copy_divide_fusion
  173.6 2.7 copy-done.1
  176.3 2.2 fusion.38
  178.4 3.5 collective-permute-start.2
  182.0 1.9 collective-permute-start.3
  184.5 17.9 %collective-permute-done.2 = f32[128,7,512]{2,0,1:T(8,128)S(1)} collective-permute-done((f32[128,7,512]{2,0,1:T(8,128)}, f32[128,7,512]{2,0,1:T(8,128)S(1)}, u32[]{:S(2)}, u32[]{:S(2)}) %collective-permute-start.2) | collective-permute-done | bytes 1835040 | tf_op jit(solution)/shard_map/ppermute | solution.py:17
  202.4 4.4 collective-permute-done.3
  206.8 11.2 %select_maximum_fusion = f32[256,38,512]{2,0,1:T(8,128)} fusion(f32[128,7,512]{2,0,1:T(8,128)} %collective-permute-done.3, f32[128,24,512]{2,0,1:T(8,128)} %copy-done.1, f32[128,7,512]{2,0,1:T(8,128)S(1)} %collective-permute-done.2), kind=kLoop, calls=%fused_computation.2 | loop fusion | flops 39845888 | bytes 29884416 | tf_op jit(solution)/shard_map/concatenate | solution.py:15
  218.0 9.5 %slice_bitcast_fusion = f32[1,128,38,512]{3,1,2,0:T(8,128)} fusion(f32[256,38,512]{2,0,1:T(8,128)} %select_maximum_fusion), kind=kLoop, calls=%fused_computation.11 | loop fusion | bytes 19922944 | tf_op jit(solution)/shard_map/reshape | solution.py:54
  227.6 9.8 %fusion.30 = f32[128,38,512]{2,0,1:T(8,128)S(1)} fusion(f32[1,128,38,512]{3,1,2,0:T(8,128)} %slice_bitcast_fusion, f32[128,158]{0,1:T(8,128)S(1)} %get-tuple-element.5), kind=kOutput, calls=%fused_computation.39 | convolution fusion | flops 896532480 | bytes 12468224 | tf_op jit(solution)/shard_map/jbyx,ob->joyx/dot_general | solution.py:58
  237.3 15.5 %fusion.16 = f32[128,38,512]{2,0,1:T(8,128)S(1)} fusion(f32[128,38,512]{2,0,1:T(8,128)S(1)} %fusion.30, f32[256,38,512]{2,0,1:T(8,128)} %select_maximum_fusion, f32[128,158]{0,1:T(8,128)S(1)} %get-tuple-element.5), kind=kOutput, calls=%fused_computation.31 | convolution fusion | flops 3827695616 | bytes 29949952 | tf_op jit(solution)/shard_map/jbyx,ob->joyx/dot_general | solution.py:55
  252.8 18.0 %fusion.27 = f32[128,24,512]{2,1,0:T(8,128)S(1)} fusion(f32[128,38,512]{2,0,1:T(8,128)S(1)} %fusion.16, f32[24,38]{1,0:T(8,128)S(1)} %get-tuple-element.9), kind=kOutput, calls=%fused_computation.34 | convolution fusion | flops 717225984 | bytes 16256576 | tf_op jit(solution)/shard_map/ya,zax->zyx/dot_general | solution.py:76
  270.9 6.4 %pad_slice_fusion.1 = (f32[128,24,512]{2,1,0:T(8,128)}, f32[128,24,512]{2,1,0:T(8,128)}) fusion(f32[128,24,512]{2,1,0:T(8,128)S(1)} %fusion.27), kind=kLoop, calls=%fused_computation.18 | loop fusion | bytes 18874368 | tf_op jit(solution)/shard_map/slice | solution.py:50
  277.3 6.6 %copy.87 = f32[128,24,512]{0,2,1:T(8,128)} copy(f32[128,24,512]{2,1,0:T(8,128)} %get-tuple-element.12) | data formatting | bytes 12582912 | tf_op jit(solution)/shard_map/reshape | solution.py:63
  283.8 7.6 %reshape.128 = f32[128,24,4,128]{3,2,1,0:T(4,128)} reshape(f32[128,24,512]{2,1,0:T(8,128)} %get-tuple-element.11) | data formatting | bytes 12582912 | tf_op jit(solution)/shard_map/reshape | solution.py:62
  291.4 6.5 %fusion.32 = f32[128,24,4,128]{0,3,2,1:T(8,128)S(1)} fusion(f32[128,24,4,128]{0,3,2,1:T(8,128)} %bitcast.83, f32[128,142]{0,1:T(8,128)S(1)} %get-tuple-element.7), kind=kOutput, calls=%fused_computation.45 | convolution fusion | flops 264241152 | bytes 7086080 | tf_op jit(solution)/shard_map/zyjb,ob->zyjo/dot_general | solution.py:67
  297.9 11.4 %add_multiply_fusion = f32[128,24,4,128]{0,3,2,1:T(8,128)} fusion(f32[128,24,4,128]{0,3,2,1:T(8,128)S(1)} %fusion.32, f32[]{:T(128)} %bitcast, f32[128,24,4,128]{3,2,1,0:T(4,128)S(1)} %copy-done.2, f32[128,142]{0,1:T(8,128)S(1)} %get-tuple-element.7), kind=kOutput, calls=%fused_computation.29 | convolution fusion | flops 2419064832 | bytes 18939908 | tf_op jit(solution)/shard_map/zyjb,ob->zyjo/dot_general | solution.py:64
  309.3 6.7 %copy.78 = f32[1,128,24,512]{3,2,1,0:T(8,128)} copy(f32[1,128,24,512]{1,3,2,0:T(8,128)} %bitcast.80) | data formatting | bytes 12582912 | tf_op jit(solution)/shard_map/mul | solution.py:105
  316.0 6.6 %copy.80 = f32[128,24,512]{0,2,1:T(8,128)} copy(f32[128,24,512]{2,1,0:T(8,128)} %param.7) | data formatting | bytes 12582912 | tf_op args[0]
  322.5 0.7 reduce_sum.109
  324.0 218.1 %all-gather.2.cloned.1.call-done = f32[4,128,24,512]{3,2,1,0:T(8,128)} async-done(((f32[1,128,24,512]{3,2,1,0:T(8,128)}), f32[4,128,24,512]{3,2,1,0:T(8,128)}) %all-gather.2.cloned.1.call-update) | async-done | bytes 25165840 | tf_op jit(solution)/shard_map/all_gather | solution.py:106
  542.1 13.2 %reduce_sum.108 = f32[128,24,512]{2,1,0:T(8,128)} reduce(f32[4,128,24,512]{3,2,1,0:T(8,128)} %all-gather.2.cloned.1.call-done, f32[]{:T(128)} %constant.27.clone.1), dimensions={0}, to_apply=%region_9.10 | reduce | flops 4718592 | bytes 31457284 | tf_op jit(solution)/shard_map/reduce_sum | solution.py:106
  555.3 6.5 %copy.88 = f32[128,24,512]{0,2,1:T(8,128)} copy(f32[128,24,512]{2,1,0:T(8,128)} %reduce_sum.108) | data formatting | bytes 12582912
  561.8 8.2 %multiply_divide_fusion = f32[128,24,512]{0,2,1:T(8,128)} fusion(f32[128,24,512]{0,2,1:T(8,128)} %copy.80, f32[128,24,512]{0,2,1:T(8,128)} %copy.88, f32[]{:T(128)S(6)} %convert_element_type.25), kind=kLoop, calls=%fused_computation.28 | loop fusion | flops 3145728 | bytes 18874372 | tf_op jit(solution)/shard_map/div | solution.py:107
  570.0 6.6 %copy.81 = f32[128,24,512]{2,1,0:T(8,128)} copy(f32[128,24,512]{0,2,1:T(8,128)} %multiply_divide_fusion) | data formatting | bytes 12582912 | tf_op jit(solution)/shard_map/div | solution.py:107
  (40 shorter events, 5.2 us)
Async XLA Ops:
  13.0 2.7 copy-start
  15.7 9.8 %copy-start.4 = (f32[1,4,768,512]{3,2,1,0:T(8,128)S(1)}, f32[1,4,768,512]{3,2,1,0:T(8,128)}, u32[]{:S(2)}) copy-start(f32[1,4,768,512]{3,2,1,0:T(8,128)} %param.8) | copy-start | bytes 18874372
  17.9 37.1 %collective-permute-start = (f32[128,7,512]{2,0,1:T(8,128)}, f32[128,7,512]{2,0,1:T(8,128)S(1)}, u32[]{:S(2)}, u32[]{:S(2)}) collective-permute-start(f32[128,7,512]{2,0,1:T(8,128)} %get-tuple-element.17), channel_id=1, source_target_pairs={{0,1},{1,2},{2,3},{3,4},{4,5},{5,6},{6,7},{7,8},{8,9},{9,10},{10,1... | collective-permute-start | bytes 5505032 | tf_op jit(solution)/shard_map/ppermute | solution.py:17
  22.7 32.4 %collective-permute-start.1 = (f32[128,7,512]{2,0,1:T(8,128)}, f32[128,7,512]{2,0,1:T(8,128)}, u32[]{:S(2)}, u32[]{:S(2)}) collective-permute-start(f32[128,7,512]{2,0,1:T(8,128)} %get-tuple-element.18), channel_id=1, source_target_pairs={{1,0},{2,1},{3,2},{4,3},{5,4},{6,5},{7,6},{8,7},{9,8},{10,9},{11,1... | collective-permute-start | bytes 5505032 | tf_op jit(solution)/shard_map/ppermute | solution.py:19
  40.9 9.3 %copy-start.7 = (f32[1,31]{1,0:T(1,128)S(1)}, f32[1,31]{1,0:T(1,128)}, u32[]{:S(2)}) copy-start(f32[1,31]{1,0:T(1,128)} %param.9) | copy-start | bytes 376
  40.9 10.0 %copy-start.5 = (f32[1,15]{1,0:T(1,128)S(1)}, f32[1,15]{1,0:T(1,128)}, u32[]{:S(2)}) copy-start(f32[1,15]{1,0:T(1,128)} %param.10) | copy-start | bytes 184
  40.9 10.7 %copy-start.6 = (f32[1,15]{1,0:T(1,128)S(1)}, f32[1,15]{1,0:T(1,128)}, u32[]{:S(2)}) copy-start(f32[1,15]{1,0:T(1,128)} %param.11) | copy-start | bytes 184
  40.9 121.9 %all-to-all-start = ((f32[4,768,512]{2,0,1:T(4,128)}), f32[4,768,512]{2,0,1:T(4,128)}, u32[]{:S(2)}, u32[]{:S(2)}) async-start(f32[4,768,512]{2,0,1:T(4,128)} %pad_dynamic-slice_fusion), calls=%async_computation | async-start | bytes 12582912 | tf_op jit(solution)/shard_map/all_to_all | solution.py:91
  49.7 492.4 %all-gather.2.cloned.1.call-start = ((), (), s32[]{:S(2)}) async-start(), calls=%async_computation.1 | async-start | bytes 31457280 | tf_op jit(solution)/shard_map/all_gather | solution.py:106
  139.2 6.5 %copy-start.3 = (f32[128,24,4,128]{3,2,1,0:T(4,128)S(1)}, f32[128,24,4,128]{3,2,1,0:T(4,128)}, u32[]{:S(2)}) copy-start(f32[128,24,4,128]{3,2,1,0:T(4,128)} %reshape.123) | copy-start | bytes 18874372
  162.8 6.0 %slice-start = ((s8[6291456]{0:T(1024)(128)(4,1)}), s8[4194304]{0:T(1024)(128)(4,1)S(1)}, s32[]{:S(2)}) async-start(s8[6291456]{0:T(1024)(128)(4,1)} %bitcast.78), calls=%async_computation.2 | async-start | bytes 8388608
  167.7 1.6 slice-start.1
  173.6 2.7 copy-start.1
  176.3 7.6 %copy-start.8 = (s32[1,4]{1,0:T(1,128)S(1)}, s32[1,4]{1,0:T(1,128)}, u32[]{:S(2)}) copy-start(s32[1,4]{1,0:T(1,128)} %param.13) | copy-start | bytes 52
  178.4 24.0 %collective-permute-start.2 = (f32[128,7,512]{2,0,1:T(8,128)}, f32[128,7,512]{2,0,1:T(8,128)S(1)}, u32[]{:S(2)}, u32[]{:S(2)}) collective-permute-start(f32[128,7,512]{2,0,1:T(8,128)} %get-tuple-element.13), channel_id=1, source_target_pairs={{0,1},{1,2},{2,3},{3,4},{4,5},{5,6},{6,7},{7,8},{8,9},{9,10},{10,1... | collective-permute-start | bytes 5505032 | tf_op jit(solution)/shard_map/ppermute | solution.py:17
  182.0 24.9 %collective-permute-start.3 = (f32[128,7,512]{2,0,1:T(8,128)}, f32[128,7,512]{2,0,1:T(8,128)}, u32[]{:S(2)}, u32[]{:S(2)}) collective-permute-start(f32[128,7,512]{2,0,1:T(8,128)} %get-tuple-element.14), channel_id=1, source_target_pairs={{1,0},{2,1},{3,2},{4,3},{5,4},{6,5},{7,6},{8,7},{9,8},{10,9},{11,1... | collective-permute-start | bytes 5505032 | tf_op jit(solution)/shard_map/ppermute | solution.py:19
  291.4 6.5 %copy-start.2 = (f32[128,24,4,128]{3,2,1,0:T(4,128)S(1)}, f32[128,24,4,128]{3,2,1,0:T(4,128)}, u32[]{:S(2)}) copy-start(f32[128,24,4,128]{3,2,1,0:T(4,128)} %reshape.128) | copy-start | bytes 18874372
Sparse Core Ops, SparseCore 0:
  316.1 225.9 all-gather.1
